TPU v7x, 512 devices: a whole 4x4x16 slice. The times are simulated.
512 devices in a mesh: feat: 64 (over x, z_hi, y, core), tok: 8 (over z_lo).
Axes of the slice: x: 4, y: 4, z: 16 (z_hi: 2, z_lo: 8; z = z_hi * 8 + z_lo), core: 2. Of those that a mesh axis runs over, the one named last changes fastest.
Arguments:
- features: bfloat16 [1024, 131072], P('tok', 'feat'), may hold values from -6 to 6
- signs: int32 [131072], P('feat'), may hold values from -1 to 1, as said below
- columns: int32 [1024], replicated, may hold values from 0 to 131071, as said below
- labels: int32 [1024, 1], P('tok'), may hold values from 0 to 31; in each aligned block of 128 rows (0 to 127, 128 to 255, ...) at most 8 rows name the same one
Outputs:
- gram: float32 [32, 1024, 1024], P('tok', 'feat')
Inputs may be any that keep to these rules, and one draw needn't show every extreme that they name: `signs`: every entry is -1 or 1. `columns`: the 1024 indices are distinct. `labels`: among the rows of one device no concept appears more than 8 times.
All inputs are finite; a program needn't handle non-finite values.
Results may differ from a plain program's by a relative error of at most 0.004.
Values may be sent and summed in bfloat16 or wider, within the bound.
A program may use at most 64 MiB of HBM per device.

v0:
```python
import math
import jax
import jax.numpy as jnp
from jax import lax
from jax.sharding import PartitionSpec as P

C = 32


def from_partner(array, axis, distance):
    return lax.ppermute(array, axis, [(i, i ^ 1 << distance) for i in range(lax.axis_size(axis))])


def bit_parity(number, bit_count):
    total = jnp.zeros_like(number)
    for position in range(bit_count):
        total = total ^ number >> position & 1
    return total


def sylvester(order, dtype):
    index = lax.iota(jnp.int32, order)
    parity = bit_parity(index[:, None] & index[None, :], order.bit_length())
    return (1 - 2 * parity).astype(dtype)


def body(features, signs, columns, labels):
    rows, width = features.shape
    feat_count = lax.axis_size("feat")
    feat_index = lax.axis_index("feat")
    tok_count = lax.axis_size("tok")
    kept = columns.shape[0]
    shard_cols = kept // feat_count
    flat_labels = labels[:, 0]
    signed = features * signs.astype(jnp.bfloat16)[None, :]
    transformed = jnp.dot(
        signed, sylvester(width, jnp.bfloat16), preferred_element_type=jnp.float32
    )
    local_col = columns % width
    owner = columns // width
    sections = feat_count.bit_length() - 1
    for section in range(sections):
        partner = from_partner(transformed, "feat", section)
        upper = feat_index >> section & 1 == 1
        transformed = jnp.where(upper, partner - transformed, transformed + partner)
    picked = jnp.take(transformed, local_col, axis=1)
    owned = (owner == feat_index)[None, :]
    combined = lax.psum(jnp.where(owned, picked, 0.0), "feat")
    sketch = (combined * (1.0 / math.sqrt(width * feat_count))).astype(jnp.bfloat16)
    factor = C / (rows * tok_count)
    own_rows = lax.dynamic_slice_in_dim(sketch, feat_index * shard_cols, shard_cols, 1)
    wanted = lax.iota(jnp.int32, C // tok_count * lax.axis_size("tok"))
    onehot = (flat_labels[:, None] == wanted[None, :]).astype(jnp.bfloat16)
    weighted = (onehot[:, :, None] * own_rows[:, None, :]).reshape(
        rows, C // tok_count * lax.axis_size("tok") * shard_cols
    )
    partial_gram = jnp.einsum("rm,rk->mk", weighted, sketch, preferred_element_type=jnp.float32)
    return lax.psum_scatter(
        partial_gram.reshape(C // tok_count * lax.axis_size("tok"), shard_cols, kept) * factor,
        "tok",
        scatter_dimension=0,
        tiled=True,
    )


def solution(mesh):
    in_specs = (P("tok", "feat"), P("feat"), P(), P("tok", None))
    out_specs = P("tok", "feat", None)
    return jax.shard_map(body, mesh=mesh, in_specs=in_specs, out_specs=out_specs, check_vma=False)
```

profile of v0, /device:TPU:12, one launch (start us, length us, event | category | flops | bytes accessed | tf_op | source)
XLA Modules:
  0.0 1409.9 jit_solution(11742431662747528848)
XLA Ops:
  6.5 0.7 convert_element_type.17
  7.2 23.5 %fusion = f32[128,2048]{1,0:T(8,128)S(1)} fusion(bf16[128,2048]{1,0:T(8,128)(2,1)} %param.4, bf16[2048]{0:T(1024)(128)(2,1)S(1)} %convert_element_type.17), kind=kOutput, calls=%fused_computation.2 | convolution fusion | flops 1237581824 | bytes 1576960 | tf_op jit(solution)/shard_map/dot_general | solution.py:36
  30.8 1.9 collective-permute-start
  32.7 2.6 collective-permute-done
  35.5 2.4 collective-permute-start.1
  37.8 24.7 %collective-permute-done.1 = f32[128,2048]{1,0:T(8,128)S(1)} collective-permute-done((f32[128,2048]{1,0:T(8,128)S(1)}, f32[128,2048]{1,0:T(8,128)S(1)}, u32[]{:S(2)}, u32[]{:S(2)}) %collective-permute-start.1) | collective-permute-done | bytes 1048608 | tf_op jit(solution)/shard_map/ppermute | solution.py:11
  62.6 0.1 add_select_fusion.4
  62.7 4.2 collective-permute-start.2
  66.9 23.6 %collective-permute-done.2 = f32[128,2048]{1,0:T(8,128)S(1)} collective-permute-done((f32[128,2048]{1,0:T(8,128)S(1)}, f32[128,2048]{1,0:T(8,128)S(1)}, u32[]{:S(2)}, u32[]{:S(2)}) %collective-permute-start.2) | collective-permute-done | bytes 1048608 | tf_op jit(solution)/shard_map/ppermute | solution.py:11
  90.6 15.7 %collective-permute-start.3 = (f32[128,2048]{1,0:T(8,128)S(1)}, f32[128,2048]{1,0:T(8,128)S(1)}, u32[]{:S(2)}, u32[]{:S(2)}) collective-permute-start(f32[128,2048]{1,0:T(8,128)S(1)} %add_select_fusion.3), channel_id=1, source_target_pairs={{0,64},{8,72},{16,80},{24,88},{32,96},{40,104},{48,112},{56,120},{... | collective-permute-start | bytes 3145736 | tf_op jit(solution)/shard_map/ppermute | solution.py:11
  106.4 35.5 %collective-permute-done.3 = f32[128,2048]{1,0:T(8,128)S(1)} collective-permute-done((f32[128,2048]{1,0:T(8,128)S(1)}, f32[128,2048]{1,0:T(8,128)S(1)}, u32[]{:S(2)}, u32[]{:S(2)}) %collective-permute-start.3) | collective-permute-done | bytes 1048608 | tf_op jit(solution)/shard_map/ppermute | solution.py:11
  141.9 0.1 add_select_fusion.2
  142.1 3.1 collective-permute-start.4
  145.2 21.3 %collective-permute-done.4 = f32[128,2048]{1,0:T(8,128)S(1)} collective-permute-done((f32[128,2048]{1,0:T(8,128)S(1)}, f32[128,2048]{1,0:T(8,128)S(1)}, u32[]{:S(2)}, u32[]{:S(2)}) %collective-permute-start.4) | collective-permute-done | bytes 1048608 | tf_op jit(solution)/shard_map/ppermute | solution.py:11
  166.6 14.8 %collective-permute-start.5 = (f32[128,2048]{1,0:T(8,128)S(1)}, f32[128,2048]{1,0:T(8,128)S(1)}, u32[]{:S(2)}, u32[]{:S(2)}) collective-permute-start(f32[128,2048]{1,0:T(8,128)S(1)} %add_select_fusion.1), channel_id=1, source_target_pairs={{0,256},{8,264},{16,272},{24,280},{32,288},{40,296},{48,304},{56,3... | collective-permute-start | bytes 3145736 | tf_op jit(solution)/shard_map/ppermute | solution.py:11
  181.5 20.4 %collective-permute-done.5 = f32[128,2048]{1,0:T(8,128)S(1)} collective-permute-done((f32[128,2048]{1,0:T(8,128)S(1)}, f32[128,2048]{1,0:T(8,128)S(1)}, u32[]{:S(2)}, u32[]{:S(2)}) %collective-permute-start.5) | collective-permute-done | bytes 1048608 | tf_op jit(solution)/shard_map/ppermute | solution.py:11
  202.1 0.3 copy.5
  202.4 2.8 gather_fusion
  205.3 0.2 copy.6
  205.5 0.8 select_bitcast_fusion
  206.4 1084.6 %all-reduce.2.cloned.1.call-done = f32[128,1024]{1,0:T(8,128)} async-done(((f32[128,1024]{1,0:T(8,128)}), f32[128,1024]{1,0:T(8,128)}) %all-reduce.2.cloned.1.call-update) | async-done | bytes 524304 | tf_op jit(solution)/shard_map/psum | solution.py:48
  1291.0 1.1 multiply_convert_fusion
  1292.2 1.8 convolution_multiply_fusion
  1294.0 109.1 %reduce-scatter.2.cloned.1.call-done = f32[4,16,1024]{2,1,0:T(8,128)} async-done(((f32[32,16,1024]{2,1,0:T(8,128)}), f32[4,16,1024]{2,1,0:T(8,128)}) %reduce-scatter.2.cloned.1.call-update) | async-done | bytes 262160 | tf_op jit(solution)/shard_map/reduce_scatter | solution.py:58
  (17 shorter events, 0.9 us)
Async XLA Ops:
  6.5 1284.4 %all-reduce.2.cloned.1.call-start = ((), (), s32[]{:S(2)}) async-start(), calls=%async_computation.1 | async-start | bytes 1048576 | tf_op jit(solution)/shard_map/psum | solution.py:48
  30.8 4.6 collective-permute-start
  35.5 27.1 %collective-permute-start.1 = (f32[128,2048]{1,0:T(8,128)S(1)}, f32[128,2048]{1,0:T(8,128)S(1)}, u32[]{:S(2)}, u32[]{:S(2)}) collective-permute-start(f32[128,2048]{1,0:T(8,128)S(1)} %add_select_fusion.5), channel_id=1, source_target_pairs={{0,16},{8,24},{16,0},{24,8},{32,48},{40,56},{48,32},{56,40},{64,80... | collective-permute-start | bytes 3145736 | tf_op jit(solution)/shard_map/ppermute | solution.py:11
  62.7 27.8 %collective-permute-start.2 = (f32[128,2048]{1,0:T(8,128)S(1)}, f32[128,2048]{1,0:T(8,128)S(1)}, u32[]{:S(2)}, u32[]{:S(2)}) collective-permute-start(f32[128,2048]{1,0:T(8,128)S(1)} %add_select_fusion.4), channel_id=1, source_target_pairs={{0,32},{8,40},{16,48},{24,56},{32,0},{40,8},{48,16},{56,24},{64,96... | collective-permute-start | bytes 3145736 | tf_op jit(solution)/shard_map/ppermute | solution.py:11
  90.6 51.2 %collective-permute-start.3 = (f32[128,2048]{1,0:T(8,128)S(1)}, f32[128,2048]{1,0:T(8,128)S(1)}, u32[]{:S(2)}, u32[]{:S(2)}) collective-permute-start(f32[128,2048]{1,0:T(8,128)S(1)} %add_select_fusion.3), channel_id=1, source_target_pairs={{0,64},{8,72},{16,80},{24,88},{32,96},{40,104},{48,112},{56,120},{... | collective-permute-start | bytes 3145736 | tf_op jit(solution)/shard_map/ppermute | solution.py:11
  142.0 39.4 %copy-start = (s32[1024]{0:T(1024)S(1)}, s32[1024]{0:T(1024)}, u32[]{:S(2)}) copy-start(s32[1024]{0:T(1024)} %param.6) | copy-start | bytes 12292
  142.1 24.4 %collective-permute-start.4 = (f32[128,2048]{1,0:T(8,128)S(1)}, f32[128,2048]{1,0:T(8,128)S(1)}, u32[]{:S(2)}, u32[]{:S(2)}) collective-permute-start(f32[128,2048]{1,0:T(8,128)S(1)} %add_select_fusion.2), channel_id=1, source_target_pairs={{0,128},{8,136},{16,144},{24,152},{32,160},{40,168},{48,176},{56,1... | collective-permute-start | bytes 3145736 | tf_op jit(solution)/shard_map/ppermute | solution.py:11
  166.6 35.3 %collective-permute-start.5 = (f32[128,2048]{1,0:T(8,128)S(1)}, f32[128,2048]{1,0:T(8,128)S(1)}, u32[]{:S(2)}, u32[]{:S(2)}) collective-permute-start(f32[128,2048]{1,0:T(8,128)S(1)} %add_select_fusion.1), channel_id=1, source_target_pairs={{0,256},{8,264},{16,272},{24,280},{32,288},{40,296},{48,304},{56,3... | collective-permute-start | bytes 3145736 | tf_op jit(solution)/shard_map/ppermute | solution.py:11
  205.2 1.1 copy-start.1
  206.3 1196.8 %reduce-scatter.2.cloned.1.call-start = ((), (), s32[]{:S(2)}) async-start(), calls=%async_computation.2 | async-start | bytes 2359296 | tf_op jit(solution)/shard_map/reduce_scatter | solution.py:58
Sparse Core Ops, SparseCore 0:
  206.5 1084.4 all-reduce.1
  1294.1 108.9 reduce-scatter.1
where the time goes:
time: 1410 us
  waiting for transfers between devices  1320 us (94%)
  starting transfers between devices  42.2 us (3%)
  matrix products  25.3 us (2%)
    psum x1, waiting for transfers between devices, body(): combined = lax.psum(jnp.where(owned, picked, 0.0), 'feat')  1080 us
    ppermute x6, waiting for transfers between devices, from_partner(): lax.ppermute(array, axis, [(i, i ^ 1 << distance) for i in range(lax.axis...  128 us
    reduce_scatter x1, waiting for transfers between devices, body(): lax.psum_scatter(partial_gram.reshape(C // tok_count * lax.axis_size('tok...  109 us
    ppermute x6, starting transfers between devices, from_partner(): lax.ppermute(array, axis, [(i, i ^ 1 << distance) for i in range(lax.axis...  42.1 us
  transfers between devices with their start and end apart: 8, of which 8 were waited for; matrix products, arithmetic and copies ran while one was open for 0% of the time, Pallas kernels for 0%

commit v1 on v0

--- a/solution.py
+++ b/solution.py
@@ -5,6 +5,11 @@
 from jax.sharding import PartitionSpec as P
 
 C = 32
+
+
+def add_all(value, axis):
+    pieces = lax.all_gather(value, axis)
+    return jnp.sum(pieces, axis=0)
 
 
 def from_partner(array, axis, distance):
@@ -45,7 +50,7 @@
         transformed = jnp.where(upper, partner - transformed, transformed + partner)
     picked = jnp.take(transformed, local_col, axis=1)
     owned = (owner == feat_index)[None, :]
-    combined = lax.psum(jnp.where(owned, picked, 0.0), "feat")
+    combined = add_all(jnp.where(owned, picked, 0.0), "feat")
     sketch = (combined * (1.0 / math.sqrt(width * feat_count))).astype(jnp.bfloat16)
     factor = C / (rows * tok_count)
     own_rows = lax.dynamic_slice_in_dim(sketch, feat_index * shard_cols, shard_cols, 1)

time: 1410 us -> 767 us (0.54)
  the two profiles are of different devices: /device:TPU:12 before, /device:TPU:4 now
where the time goes in v1:
time: 767 us
  waiting for transfers between devices  655 us (85%)
  starting transfers between devices  54.9 us (7%)
  matrix products  25.3 us (3%)
  other arithmetic  13.8 us (2%)
  between operations  13.6 us (2%)
    all_gather x1, waiting for transfers between devices, add_all(): pieces = lax.all_gather(value, axis)  438 us
    ppermute x6, waiting for transfers between devices, from_partner(): lax.ppermute(array, axis, [(i, i ^ 1 << distance) for i in range(lax.axis...  126 us
    reduce_scatter x1, waiting for transfers between devices, body(): lax.psum_scatter(partial_gram.reshape(C // tok_count * lax.axis_size('tok...  89.7 us
    ppermute x6, starting transfers between devices, from_partner(): lax.ppermute(array, axis, [(i, i ^ 1 << distance) for i in range(lax.axis...  54.8 us
    dot_general x1, matrix products, body(): jnp.dot(signed, sylvester(width, jnp.bfloat16), preferred_element_type=jn...  23.5 us
  transfers between devices with their start and end apart: 8, of which 8 were waited for; matrix products, arithmetic and copies ran while one was open for 0% of the time, Pallas kernels for 0%

profile of v1, /device:TPU:4, one launch (start us, length us, event | category | flops | bytes accessed | tf_op | source)
XLA Modules:
  0.0 766.6 jit_solution(306146808236919150)
XLA Ops:
  6.5 0.7 convert_element_type.17
  7.2 23.5 %fusion = f32[128,2048]{1,0:T(8,128)S(1)} fusion(bf16[128,2048]{1,0:T(8,128)(2,1)} %param.4, bf16[2048]{0:T(1024)(128)(2,1)S(1)} %convert_element_type.17), kind=kOutput, calls=%fused_computation.2 | convolution fusion | flops 1237581824 | bytes 1576960 | tf_op jit(solution)/shard_map/dot_general | solution.py:41
  30.8 1.9 collective-permute-start
  32.7 2.6 collective-permute-done
  35.5 3.5 collective-permute-start.1
  39.0 23.6 %collective-permute-done.1 = f32[128,2048]{1,0:T(8,128)S(1)} collective-permute-done((f32[128,2048]{1,0:T(8,128)S(1)}, f32[128,2048]{1,0:T(8,128)S(1)}, u32[]{:S(2)}, u32[]{:S(2)}) %collective-permute-start.1) | collective-permute-done | bytes 1048608 | tf_op jit(solution)/shard_map/ppermute | solution.py:16
  62.6 0.1 add_select_fusion.4
  62.7 5.3 collective-permute-start.2
  68.1 22.4 %collective-permute-done.2 = f32[128,2048]{1,0:T(8,128)S(1)} collective-permute-done((f32[128,2048]{1,0:T(8,128)S(1)}, f32[128,2048]{1,0:T(8,128)S(1)}, u32[]{:S(2)}, u32[]{:S(2)}) %collective-permute-start.2) | collective-permute-done | bytes 1048608 | tf_op jit(solution)/shard_map/ppermute | solution.py:16
  90.7 15.7 %collective-permute-start.3 = (f32[128,2048]{1,0:T(8,128)S(1)}, f32[128,2048]{1,0:T(8,128)S(1)}, u32[]{:S(2)}, u32[]{:S(2)}) collective-permute-start(f32[128,2048]{1,0:T(8,128)S(1)} %add_select_fusion.3), channel_id=1, source_target_pairs={{0,64},{8,72},{16,80},{24,88},{32,96},{40,104},{48,112},{56,120},{... | collective-permute-start | bytes 3145736 | tf_op jit(solution)/shard_map/ppermute | solution.py:16
  106.4 35.5 %collective-permute-done.3 = f32[128,2048]{1,0:T(8,128)S(1)} collective-permute-done((f32[128,2048]{1,0:T(8,128)S(1)}, f32[128,2048]{1,0:T(8,128)S(1)}, u32[]{:S(2)}, u32[]{:S(2)}) %collective-permute-start.3) | collective-permute-done | bytes 1048608 | tf_op jit(solution)/shard_map/ppermute | solution.py:16
  142.1 3.1 collective-permute-start.4
  145.2 21.3 %collective-permute-done.4 = f32[128,2048]{1,0:T(8,128)S(1)} collective-permute-done((f32[128,2048]{1,0:T(8,128)S(1)}, f32[128,2048]{1,0:T(8,128)S(1)}, u32[]{:S(2)}, u32[]{:S(2)}) %collective-permute-start.4) | collective-permute-done | bytes 1048608 | tf_op jit(solution)/shard_map/ppermute | solution.py:16
  166.6 25.2 %collective-permute-start.5 = (f32[128,2048]{1,0:T(8,128)S(1)}, f32[128,2048]{1,0:T(8,128)S(1)}, u32[]{:S(2)}, u32[]{:S(2)}) collective-permute-start(f32[128,2048]{1,0:T(8,128)S(1)} %add_select_fusion.1), channel_id=1, source_target_pairs={{0,256},{8,264},{16,272},{24,280},{32,288},{40,296},{48,304},{56,3... | collective-permute-start | bytes 3145736 | tf_op jit(solution)/shard_map/ppermute | solution.py:16
  191.9 21.0 %collective-permute-done.5 = f32[128,2048]{1,0:T(8,128)S(1)} collective-permute-done((f32[128,2048]{1,0:T(8,128)S(1)}, f32[128,2048]{1,0:T(8,128)S(1)}, u32[]{:S(2)}, u32[]{:S(2)}) %collective-permute-start.5) | collective-permute-done | bytes 1048608 | tf_op jit(solution)/shard_map/ppermute | solution.py:16
  213.1 0.3 copy.7
  213.4 2.8 gather_fusion
  216.2 0.3 fusion.1
  216.6 1.0 copy.8
  217.7 438.5 %all-gather.2.cloned.1.call-done = f32[64,128,1024]{2,1,0:T(8,128)} async-done(((f32[1,128,1024]{2,1,0:T(8,128)}), f32[64,128,1024]{2,1,0:T(8,128)}) %all-gather.2.cloned.1.call-update) | async-done | bytes 33554448 | tf_op jit(solution)/shard_map/all_gather | solution.py:11
  656.2 11.8 %reduce_sum.9 = f32[128,1024]{1,0:T(8,128)S(1)} reduce(f32[64,128,1024]{2,1,0:T(8,128)} %all-gather.2.cloned.1.call-done, f32[]{:T(128)} %constant.79.clone.1), dimensions={0}, to_apply=%region_0.1 | reduce | flops 8257536 | bytes 34078724 | tf_op jit(solution)/shard_map/reduce_sum | solution.py:12
  668.0 0.2 copy.13
  668.2 1.8 convolution_multiply_fusion
  670.0 89.7 %reduce-scatter.2.cloned.1.call-done = f32[4,16,1024]{2,1,0:T(8,128)} async-done(((f32[32,16,1024]{2,1,0:T(8,128)}), f32[4,16,1024]{2,1,0:T(8,128)}) %reduce-scatter.2.cloned.1.call-update) | async-done | bytes 262160 | tf_op jit(solution)/shard_map/reduce_scatter | solution.py:63
  (18 shorter events, 0.9 us)
Async XLA Ops:
  6.5 649.6 %all-gather.2.cloned.1.call-start = ((), (), s32[]{:S(2)}) async-start(), calls=%async_computation.1 | async-start | bytes 34078720 | tf_op jit(solution)/shard_map/all_gather | solution.py:11
  7.2 184.7 %copy-start = (s32[1024]{0:T(1024)S(1)}, s32[1024]{0:T(1024)}, u32[]{:S(2)}) copy-start(s32[1024]{0:T(1024)} %param.6) | copy-start | bytes 12292
  30.8 186.9 %copy-start.1 = (s32[128,1]{0,1:T(1,128)S(1)}, s32[128,1]{0,1:T(1,128)}, u32[]{:S(2)}) copy-start(s32[128,1]{0,1:T(1,128)} %param.7) | copy-start | bytes 1540
  30.8 4.6 collective-permute-start
  35.5 27.1 %collective-permute-start.1 = (f32[128,2048]{1,0:T(8,128)S(1)}, f32[128,2048]{1,0:T(8,128)S(1)}, u32[]{:S(2)}, u32[]{:S(2)}) collective-permute-start(f32[128,2048]{1,0:T(8,128)S(1)} %add_select_fusion.5), channel_id=1, source_target_pairs={{0,16},{8,24},{16,0},{24,8},{32,48},{40,56},{48,32},{56,40},{64,80... | collective-permute-start | bytes 3145736 | tf_op jit(solution)/shard_map/ppermute | solution.py:16
  62.7 27.8 %collective-permute-start.2 = (f32[128,2048]{1,0:T(8,128)S(1)}, f32[128,2048]{1,0:T(8,128)S(1)}, u32[]{:S(2)}, u32[]{:S(2)}) collective-permute-start(f32[128,2048]{1,0:T(8,128)S(1)} %add_select_fusion.4), channel_id=1, source_target_pairs={{0,32},{8,40},{16,48},{24,56},{32,0},{40,8},{48,16},{56,24},{64,96... | collective-permute-start | bytes 3145736 | tf_op jit(solution)/shard_map/ppermute | solution.py:16
  90.7 51.2 %collective-permute-start.3 = (f32[128,2048]{1,0:T(8,128)S(1)}, f32[128,2048]{1,0:T(8,128)S(1)}, u32[]{:S(2)}, u32[]{:S(2)}) collective-permute-start(f32[128,2048]{1,0:T(8,128)S(1)} %add_select_fusion.3), channel_id=1, source_target_pairs={{0,64},{8,72},{16,80},{24,88},{32,96},{40,104},{48,112},{56,120},{... | collective-permute-start | bytes 3145736 | tf_op jit(solution)/shard_map/ppermute | solution.py:16
  142.1 24.4 %collective-permute-start.4 = (f32[128,2048]{1,0:T(8,128)S(1)}, f32[128,2048]{1,0:T(8,128)S(1)}, u32[]{:S(2)}, u32[]{:S(2)}) collective-permute-start(f32[128,2048]{1,0:T(8,128)S(1)} %add_select_fusion.2), channel_id=1, source_target_pairs={{0,128},{8,136},{16,144},{24,152},{32,160},{40,168},{48,176},{56,1... | collective-permute-start | bytes 3145736 | tf_op jit(solution)/shard_map/ppermute | solution.py:16
  166.6 46.3 %collective-permute-start.5 = (f32[128,2048]{1,0:T(8,128)S(1)}, f32[128,2048]{1,0:T(8,128)S(1)}, u32[]{:S(2)}, u32[]{:S(2)}) collective-permute-start(f32[128,2048]{1,0:T(8,128)S(1)} %add_select_fusion.1), channel_id=1, source_target_pairs={{0,256},{8,264},{16,272},{24,280},{32,288},{40,296},{48,304},{56,3... | collective-permute-start | bytes 3145736 | tf_op jit(solution)/shard_map/ppermute | solution.py:16
  217.6 542.1 %reduce-scatter.2.cloned.1.call-start = ((), (), s32[]{:S(2)}) async-start(), calls=%async_computation.2 | async-start | bytes 2359296 | tf_op jit(solution)/shard_map/reduce_scatter | solution.py:63
Sparse Core Ops, SparseCore 0:
  217.7 438.3 all-gather.1
  670.2 89.5 reduce-scatter.1
